TPU v7x, 256 devices: a whole 4x4x8 slice. The times are simulated.
256 devices in a mesh: blk: 32 (over y_lo, z, core), grp: 8 (over y_hi, x).
Axes of the slice: x: 4, y: 4 (y_hi: 2, y_lo: 2; y = y_hi * 2 + y_lo), z: 8, core: 2. Of those that a mesh axis runs over, the one named last changes fastest.
Arguments:
- matrix_sat: float32 [2048, 131072], P('grp', 'blk'), may hold values from -0.046875 to 0.046875
- matrix_ter: float32 [2048, 131072], P('grp', 'blk'), may hold values from -0.046875 to 0.046875
- probes: float32 [16, 131072], P(None, 'blk'), may hold values from -6 to 6
Outputs:
- row_part: float32 [2, 16, 2048], P(None, None, 'grp')
- column_part: float32 [2, 16, 131072], P(None, None, ('blk', 'grp'))
- trace_terms: float32 [2, 16], replicated
All inputs are finite; a program needn't handle non-finite values.
Results may differ from a plain program's by a relative error of at most 0.000096.
Values sent between devices are 32-bit elements; how exact they have to be, the bound alone decides.
No kernel may reach another device: no remote copies, remote signals or barrier semaphores. Data moves between devices by JAX's collectives and lax.ppermute only.
A program may use at most 64 MiB of HBM per device.

v0:
```python
import jax
import jax.numpy as jnp
from jax import lax
from jax.sharding import Mesh
from jax.sharding import PartitionSpec as P

BLK = ("blk_0", "blk_1", "blk_2")
GRP = ("grp_0", "grp_1")
BLK_GRP = ("blk_0", "blk_1", "blk_2", "grp_0", "grp_1")


def from_root(shard, axis, root):
    return lax.dynamic_index_in_dim(lax.all_gather(shard, axis), root, 0, keepdims=False)


def one_axis_at_a_time(shard, axes):
    for axis in axes:
        shard = lax.psum(shard, axis)
    return shard


def total_of_pieces(shard, axis):
    return lax.all_gather(shard, axis).sum(0)


def cut_along(shard, dim, size):
    dims = shard.shape
    blocks = shard.reshape(*dims[:dim], size, dims[dim] // size, *dims[dim + 1 :])
    return jnp.moveaxis(blocks, dim, 0)


def summed_on_arrival(shard, axis, dim):
    blocks = cut_along(shard, dim, lax.axis_size(axis))
    arrived = lax.all_to_all(blocks, axis, split_axis=0, concat_axis=0, tiled=True)
    return arrived.sum(axis=0)


def shards(matrix_sat, matrix_ter, probes):
    rows_dev, cols_dev = matrix_sat.shape
    column_index = lax.axis_index(BLK)
    row_index = lax.axis_index(GRP)
    row_ids = row_index * rows_dev + lax.broadcasted_iota(jnp.int32, (rows_dev, cols_dev), 0)
    col_ids = column_index * cols_dev + lax.broadcasted_iota(jnp.int32, (rows_dev, cols_dev), 1)
    upper_mask = col_ids >= row_ids
    strict_mask = col_ids > row_ids
    mine = lax.dynamic_slice_in_dim(probes, row_index * rows_dev, rows_dev, 1)
    slab_probes = from_root(mine, BLK, 0)
    hp = lax.Precision.HIGHEST
    direct_list = []
    mirror_list = []
    for matrix in (matrix_sat, matrix_ter):
        masked_upper = jnp.where(upper_mask, matrix, 0.0)
        masked_strict = jnp.where(strict_mask, matrix, 0.0)
        direct_list.append(
            lax.dot_general(probes, masked_upper, (((1,), (1,)), ((), ())), precision=hp)
        )
        mirror_list.append(jnp.dot(slab_probes, masked_strict, precision=hp))
    direct_terms = jnp.stack(direct_list)
    mirror_terms = jnp.stack(mirror_list)
    early_local = jnp.sum(slab_probes[None] * direct_terms, axis=2) + jnp.sum(
        probes[None] * mirror_terms, axis=2
    )
    early_trace = one_axis_at_a_time(early_local, BLK_GRP)
    row_part = total_of_pieces(direct_terms, BLK)
    column_part = summed_on_arrival(mirror_terms, GRP, 2)
    return (row_part, column_part, early_trace)


def solution(mesh):
    split = Mesh(mesh.devices.reshape(2, 8, 2, 2, 4), ("blk_0", "blk_1", "blk_2", "grp_0", "grp_1"))
    in_specs = (P(GRP, BLK), P(GRP, BLK), P(None, BLK))
    out_specs = (P(None, None, GRP), P(None, None, BLK_GRP), P())
    return jax.shard_map(
        shards, mesh=split, in_specs=in_specs, out_specs=out_specs, check_vma=False
    )
```

profile of v0, /device:TPU:1, one launch (start us, length us, event | category | flops | bytes accessed | tf_op | source)
XLA Modules:
  0.0 126.6 jit_solution(13252278011082796991)
XLA Ops:
  7.2 0.0 copy-start.2
  7.2 0.0 all-gather.4.cloned.1.call-start
  7.3 0.0 copy-start
  7.3 0.9 constant_dynamic-slice_fusion
  8.2 5.8 %fusion.16 = f32[1,16,256]{2,1,0:T(8,128)S(1)} fusion(f32[16,4096]{1,0:T(8,128)} %param.5, f32[256,4096]{1,0:T(8,128)} %param.4, s32[4096]{0:T(1024)S(1)} %iota_add_fusion, s32[256]{0:T(256)S(1)} %iota_add_fusion.1), kind=kOutput, calls=%fused_computation.20 | convolution fusion | flops 203423744 | bytes 4490240 | tf_op jit(solution)/shard_map/dot_general | solution.py:55
  14.0 0.0 copy-done.2
  14.0 0.0 copy-done
  14.0 3.5 %fusion.17 = f32[1,16,256]{2,1,0:T(8,128)S(1)} fusion(f32[16,4096]{1,0:T(8,128)S(1)} %copy-done.2, f32[256,4096]{1,0:T(8,128)S(1)} %copy-done, s32[4096]{0:T(1024)S(1)} %iota_add_fusion, s32[256]{0:T(256)S(1)} %iota_add_fusion.1), kind=kOutput, calls=%fused_computation.21 | convolution fusion | flops 203423744 | bytes 4490240 | tf_op jit(solution)/shard_map/dot_general | solution.py:55
  17.5 40.0 %all-gather.1 = f32[512,256]{1,0:T(8,128)S(1)} all-gather(f32[16,256]{1,0:T(8,128)S(1)} %constant_dynamic-slice_fusion), channel_id=3, replica_groups=mesh['blk_0'=2,'blk_1'=8,'blk_2'=2,'grp_0'=2,'grp_1'=4] {'blk_0','blk_1'..., dimensions={0}, use_global_device_ids=true | all-gather | bytes 540672 | tf_op jit(solution)/shard_map/all_gather | solution.py:13
  57.5 0.6 multiply_reduce_fusion
  58.1 0.0 all-gather.4.cloned.1.call-update
  58.1 0.0 copy-start.1
  58.1 4.7 %fusion.2 = f32[16,4096]{1,0:T(8,128)S(1)} fusion(f32[256,4096]{1,0:T(8,128)} %param.3, s32[4096]{0:T(1024)S(1)} %iota_add_fusion, s32[256]{0:T(256)S(1)} %iota_add_fusion.1, f32[512,256]{1,0:T(8,128)S(1)} %all-gather.1), kind=kOutput, calls=%fused_computation.6 | convolution fusion | flops 203423744 | bytes 4490240 | tf_op jit(solution)/shard_map/dot_general | solution.py:57
  62.8 0.2 copy.8
  63.0 0.2 copy.6
  63.1 0.0 copy-done.1
  63.2 2.4 %fusion.3 = f32[16,4096]{1,0:T(8,128)S(1)} fusion(f32[256,4096]{1,0:T(8,128)S(1)} %copy-done.1, s32[4096]{0:T(1024)S(1)} %iota_add_fusion, s32[256]{0:T(256)S(1)} %iota_add_fusion.1, f32[512,256]{1,0:T(8,128)S(1)} %all-gather.1), kind=kOutput, calls=%fused_computation.7 | convolution fusion | flops 203423744 | bytes 4490240 | tf_op jit(solution)/shard_map/dot_general | solution.py:57
  65.5 0.2 copy.9
  65.7 0.2 copy.7
  65.9 0.9 maximum_bitcast_fusion
  66.7 6.4 %all-to-all-start = ((f32[8,2,16,512]{3,2,1,0:T(8,128)}), f32[8,2,16,512]{3,2,1,0:T(8,128)S(1)}, u32[]{:S(2)}, u32[]{:S(2)}) async-start(f32[8,2,16,512]{3,2,1,0:T(8,128)} %maximum_bitcast_fusion), calls=%async_computation | async-start | bytes 1048576 | tf_op jit(solution)/shard_map/all_to_all | solution.py:34
  73.1 0.1 fusion.18
  73.2 4.1 %psum.35 = f32[2,16]{1,0:T(2,128)S(1)} all-reduce(f32[2,16]{1,0:T(2,128)S(1)} %add.49), channel_id=1, replica_groups=mesh['blk_0'=2,'blk_1'=8,'blk_2'=2,'grp_0'=2,'grp_1'=4] {'blk_0'}, use_global_device_ids=true, to_apply=%region_4.5 | all-reduce | flops 32 | bytes 256 | tf_op jit(solution)/shard_map/psum | solution.py:18
  77.3 11.3 %psum.36 = f32[2,16]{1,0:T(2,128)S(1)} all-reduce(f32[2,16]{1,0:T(2,128)S(1)} %psum.35), channel_id=1, replica_groups=mesh['blk_0'=2,'blk_1'=8,'blk_2'=2,'grp_0'=2,'grp_1'=4] {'blk_1'}, use_global_device_ids=true, to_apply=%region_5.6 | all-reduce | flops 32 | bytes 256 | tf_op jit(solution)/shard_map/psum | solution.py:18
  88.6 6.9 %psum.37 = f32[2,16]{1,0:T(2,128)S(1)} all-reduce(f32[2,16]{1,0:T(2,128)S(1)} %psum.36), channel_id=1, replica_groups=mesh['blk_0'=2,'blk_1'=8,'blk_2'=2,'grp_0'=2,'grp_1'=4] {'blk_2'}, use_global_device_ids=true, to_apply=%region_6.7 | all-reduce | flops 32 | bytes 256 | tf_op jit(solution)/shard_map/psum | solution.py:18
  95.5 6.2 %psum.38 = f32[2,16]{1,0:T(2,128)S(1)} all-reduce(f32[2,16]{1,0:T(2,128)S(1)} %psum.37), channel_id=1, replica_groups=mesh['blk_0'=2,'blk_1'=8,'blk_2'=2,'grp_0'=2,'grp_1'=4] {'grp_0'}, use_global_device_ids=true, to_apply=%region_7.8 | all-reduce | flops 32 | bytes 256 | tf_op jit(solution)/shard_map/psum | solution.py:18
  101.7 10.4 %psum.39 = f32[2,16]{1,0:T(2,128)} all-reduce(f32[2,16]{1,0:T(2,128)S(1)} %psum.38), channel_id=1, replica_groups=mesh['blk_0'=2,'blk_1'=8,'blk_2'=2,'grp_0'=2,'grp_1'=4] {'grp_1'}, use_global_device_ids=true, to_apply=%region_8.9 | all-reduce | flops 32 | bytes 256 | tf_op jit(solution)/shard_map/psum | solution.py:18
  112.1 0.0 all-to-all-done
  112.1 0.7 reduce_sum.37
  112.7 5.1 %all-gather.4.cloned.1.call-done = f32[64,16,256]{2,1,0:T(8,128)} async-done(((f32[2,16,256]{2,1,0:T(8,128)}), f32[64,16,256]{2,1,0:T(8,128)}) %all-gather.4.cloned.1.call-update) | async-done | bytes 1048592 | tf_op jit(solution)/shard_map/all_gather | solution.py:23
  117.8 1.9 %reduce_sum.36 = f32[2,16,256]{2,1,0:T(8,128)} reduce(f32[32,2,16,256]{3,2,1,0:T(8,128)} %bitcast.25, f32[]{:T(128)} %constant.37.clone.1), dimensions={0}, to_apply=%region_0.1 | reduce | flops 253952 | bytes 1081348 | tf_op jit(solution)/shard_map/reduce_sum | solution.py:23
  (4 shorter events, 0.0 us)
Async XLA Ops:
  7.2 6.8 %copy-start.2 = (f32[16,4096]{1,0:T(8,128)S(1)}, f32[16,4096]{1,0:T(8,128)}, u32[]{:S(2)}) copy-start(f32[16,4096]{1,0:T(8,128)} %param.5) | copy-start | bytes 786436
  7.2 110.7 %all-gather.4.cloned.1.call-start = ((), (), s32[]{:S(2)}) async-start(), calls=%async_computation.1 | async-start | bytes 1081344 | tf_op jit(solution)/shard_map/all_gather | solution.py:23
  7.3 6.8 %copy-start = (f32[256,4096]{1,0:T(8,128)S(1)}, f32[256,4096]{1,0:T(8,128)}, u32[]{:S(2)}) copy-start(f32[256,4096]{1,0:T(8,128)} %param.3) | copy-start | bytes 12582916
  58.1 5.0 %copy-start.1 = (f32[256,4096]{1,0:T(8,128)S(1)}, f32[256,4096]{1,0:T(8,128)}, u32[]{:S(2)}) copy-start(f32[256,4096]{1,0:T(8,128)} %param.4) | copy-start | bytes 12582916
  66.7 45.3 %all-to-all-start = ((f32[8,2,16,512]{3,2,1,0:T(8,128)}), f32[8,2,16,512]{3,2,1,0:T(8,128)S(1)}, u32[]{:S(2)}, u32[]{:S(2)}) async-start(f32[8,2,16,512]{3,2,1,0:T(8,128)} %maximum_bitcast_fusion), calls=%async_computation | async-start | bytes 1048576 | tf_op jit(solution)/shard_map/all_to_all | solution.py:34
Sparse Core Ops, SparseCore 0:
  58.2 59.5 all-gather.3
where the time goes:
time: 127 us
  blocking collectives  78.8 us (62%)
  matrix products  16.4 us (13%)
  between operations  14.1 us (11%)
  starting transfers between devices  6.39 us (5%)
  waiting for transfers between devices  5.13 us (4%)
  other arithmetic  4.2 us (3%)
  local copies, waits for them, and re-layouts  1.54 us (1%)
    all_gather x1, blocking collectives, from_root(): lax.all_gather(shard, axis)  40 us
    psum x5, blocking collectives, one_axis_at_a_time(): shard = lax.psum(shard, axis)  38.8 us
    dot_general x2, matrix products, shards(): lax.dot_general(probes, masked_upper, (((1,), (1,)), ((), ())), precision...  9.3 us
    dot_general x2, matrix products, shards(): mirror_list.append(jnp.dot(slab_probes, masked_strict, precision=hp))  7.08 us
    all_to_all x1, starting transfers between devices, summed_on_arrival(): lax.all_to_all(blocks, axis, split_axis=0, concat_axis=0, tiled=True)  6.36 us
    all_gather x1, waiting for transfers between devices, total_of_pieces(): return lax.all_gather(shard, axis).sum(0)  5.11 us
  transfers between devices with their start and end apart: 2, of which 1 were waited for; matrix products, arithmetic and copies ran while one was open for 7% of the time, Pallas kernels for 0%

commit v1 on v0

--- a/solution.py
+++ b/solution.py
@@ -15,7 +15,7 @@
 
 def one_axis_at_a_time(shard, axes):
     for axis in axes:
-        shard = lax.psum(shard, axis)
+        shard = jnp.sum(lax.all_gather(shard, axis), axis=0)
     return shard
 
 

time: 127 us -> 127 us (level)
  blocking collectives: 78.8 us -> 75.2 us
  waiting for transfers between devices: 5.13 us -> 8.1 us
    psum x5 -> x0, blocking collectives: 38.8 us -> none  [one_axis_at_a_time(): shard = lax.psum(shard, axis)]
    all_gather x0 -> x5, blocking collectives: none -> 35.2 us  [one_axis_at_a_time(): shard = jnp.sum(lax.all_gather(shard, axis), axis=0)]
    all_gather x1, waiting for transfers between devices: 5.11 us -> 8.08 us  [total_of_pieces(): return lax.all_gather(shard, axis).sum(0)]
  transfers between devices with their start and end apart: 2 -> 2, of which waited for: 1 -> 1; matrix products, arithmetic and copies ran while one was open for 7% -> 8% of each run, Pallas kernels for 0% -> 0%
where the time goes in v1:
time: 127 us
  blocking collectives  75.2 us (59%)
  matrix products  16.4 us (13%)
  between operations  14.1 us (11%)
  waiting for transfers between devices  8.1 us (6%)
  starting transfers between devices  6.39 us (5%)
  other arithmetic  4.84 us (4%)
  local copies, waits for them, and re-layouts  1.54 us (1%)
    all_gather x1, blocking collectives, from_root(): lax.all_gather(shard, axis)  40 us
    all_gather x5, blocking collectives, one_axis_at_a_time(): shard = jnp.sum(lax.all_gather(shard, axis), axis=0)  35.2 us
    dot_general x2, matrix products, shards(): lax.dot_general(probes, masked_upper, (((1,), (1,)), ((), ())), precision...  9.3 us
    all_gather x1, waiting for transfers between devices, total_of_pieces(): return lax.all_gather(shard, axis).sum(0)  8.08 us
    dot_general x2, matrix products, shards(): mirror_list.append(jnp.dot(slab_probes, masked_strict, precision=hp))  7.08 us
    all_to_all x1, starting transfers between devices, summed_on_arrival(): lax.all_to_all(blocks, axis, split_axis=0, concat_axis=0, tiled=True)  6.36 us
  transfers between devices with their start and end apart: 2, of which 1 were waited for; matrix products, arithmetic and copies ran while one was open for 8% of the time, Pallas kernels for 0%

profile of v1, /device:TPU:1, one launch (start us, length us, event | category | flops | bytes accessed | tf_op | source)
XLA Modules:
  0.0 126.6 jit_solution(916887990187392929)
XLA Ops:
  7.2 0.0 copy-start.2
  7.2 0.0 all-gather.14.cloned.1.call-start
  7.3 0.0 copy-start
  7.3 0.9 constant_dynamic-slice_fusion
  8.2 5.8 %fusion.16 = f32[1,16,256]{2,1,0:T(8,128)S(1)} fusion(f32[16,4096]{1,0:T(8,128)} %param.5, f32[256,4096]{1,0:T(8,128)} %param.4, s32[4096]{0:T(1024)S(1)} %iota_add_fusion, s32[256]{0:T(256)S(1)} %iota_add_fusion.1), kind=kOutput, calls=%fused_computation.20 | convolution fusion | flops 203423744 | bytes 4490240 | tf_op jit(solution)/shard_map/dot_general | solution.py:55
  14.0 0.0 copy-done.2
  14.0 0.0 copy-done
  14.0 3.5 %fusion.17 = f32[1,16,256]{2,1,0:T(8,128)S(1)} fusion(f32[16,4096]{1,0:T(8,128)S(1)} %copy-done.2, f32[256,4096]{1,0:T(8,128)S(1)} %copy-done, s32[4096]{0:T(1024)S(1)} %iota_add_fusion, s32[256]{0:T(256)S(1)} %iota_add_fusion.1), kind=kOutput, calls=%fused_computation.21 | convolution fusion | flops 203423744 | bytes 4490240 | tf_op jit(solution)/shard_map/dot_general | solution.py:55
  17.5 40.0 %all-gather.1 = f32[512,256]{1,0:T(8,128)S(1)} all-gather(f32[16,256]{1,0:T(8,128)S(1)} %constant_dynamic-slice_fusion), channel_id=3, replica_groups=mesh['blk_0'=2,'blk_1'=8,'blk_2'=2,'grp_0'=2,'grp_1'=4] {'blk_0','blk_1'..., dimensions={0}, use_global_device_ids=true | all-gather | bytes 540672 | tf_op jit(solution)/shard_map/all_gather | solution.py:13
  57.5 0.6 multiply_reduce_fusion
  58.1 0.0 all-gather.14.cloned.1.call-update
  58.1 0.0 copy-start.1
  58.1 4.7 %fusion.2 = f32[16,4096]{1,0:T(8,128)S(1)} fusion(f32[256,4096]{1,0:T(8,128)} %param.3, s32[4096]{0:T(1024)S(1)} %iota_add_fusion, s32[256]{0:T(256)S(1)} %iota_add_fusion.1, f32[512,256]{1,0:T(8,128)S(1)} %all-gather.1), kind=kOutput, calls=%fused_computation.6 | convolution fusion | flops 203423744 | bytes 4490240 | tf_op jit(solution)/shard_map/dot_general | solution.py:57
  62.8 0.2 copy.8
  63.0 0.2 copy.6
  63.1 0.0 copy-done.1
  63.2 2.4 %fusion.3 = f32[16,4096]{1,0:T(8,128)S(1)} fusion(f32[256,4096]{1,0:T(8,128)S(1)} %copy-done.1, s32[4096]{0:T(1024)S(1)} %iota_add_fusion, s32[256]{0:T(256)S(1)} %iota_add_fusion.1, f32[512,256]{1,0:T(8,128)S(1)} %all-gather.1), kind=kOutput, calls=%fused_computation.7 | convolution fusion | flops 203423744 | bytes 4490240 | tf_op jit(solution)/shard_map/dot_general | solution.py:57
  65.5 0.2 copy.9
  65.7 0.2 copy.7
  65.9 0.9 maximum_bitcast_fusion
  66.7 6.4 %all-to-all-start = ((f32[8,2,16,512]{3,2,1,0:T(8,128)}), f32[8,2,16,512]{3,2,1,0:T(8,128)S(1)}, u32[]{:S(2)}, u32[]{:S(2)}) async-start(f32[8,2,16,512]{3,2,1,0:T(8,128)} %maximum_bitcast_fusion), calls=%async_computation | async-start | bytes 1048576 | tf_op jit(solution)/shard_map/all_to_all | solution.py:34
  73.1 0.1 fusion.18
  73.2 3.1 %all-gather.7 = f32[2,2,16]{2,1,0:T(2,128)S(1)} all-gather(f32[1,2,16]{2,1,0:T(2,128)S(1)} %add_bitcast_fusion), channel_id=4, replica_groups=mesh['blk_0'=2,'blk_1'=8,'blk_2'=2,'grp_0'=2,'grp_1'=4] {'blk_0'}, dimensions={0}, use_global_device_ids=true | all-gather | bytes 384 | tf_op jit(solution)/shard_map/all_gather | solution.py:18
  76.3 10.4 %all-gather.8 = f32[8,2,16]{2,1,0:T(2,128)S(1)} all-gather(f32[1,2,16]{2,1,0:T(2,128)S(1)} %bitcast.34), channel_id=5, replica_groups=mesh['blk_0'=2,'blk_1'=8,'blk_2'=2,'grp_0'=2,'grp_1'=4] {'blk_1'}, dimensions={0}, use_global_device_ids=true | all-gather | bytes 1152 | tf_op jit(solution)/shard_map/all_gather | solution.py:18
  86.8 5.9 %all-gather.9 = f32[2,2,16]{2,1,0:T(2,128)S(1)} all-gather(f32[1,2,16]{2,1,0:T(2,128)S(1)} %bitcast.35), channel_id=6, replica_groups=mesh['blk_0'=2,'blk_1'=8,'blk_2'=2,'grp_0'=2,'grp_1'=4] {'blk_2'}, dimensions={0}, use_global_device_ids=true | all-gather | bytes 384 | tf_op jit(solution)/shard_map/all_gather | solution.py:18
  92.7 4.8 %all-gather.10 = f32[2,2,16]{2,1,0:T(2,128)S(1)} all-gather(f32[1,2,16]{2,1,0:T(2,128)S(1)} %bitcast.36), channel_id=7, replica_groups=mesh['blk_0'=2,'blk_1'=8,'blk_2'=2,'grp_0'=2,'grp_1'=4] {'grp_0'}, dimensions={0}, use_global_device_ids=true | all-gather | bytes 384 | tf_op jit(solution)/shard_map/all_gather | solution.py:18
  97.6 10.9 %all-gather.11 = f32[4,2,16]{2,1,0:T(2,128)S(1)} all-gather(f32[1,2,16]{2,1,0:T(2,128)S(1)} %bitcast.37), channel_id=8, replica_groups=mesh['blk_0'=2,'blk_1'=8,'blk_2'=2,'grp_0'=2,'grp_1'=4] {'grp_1'}, dimensions={0}, use_global_device_ids=true | all-gather | bytes 640 | tf_op jit(solution)/shard_map/all_gather | solution.py:18
  108.5 0.6 reduce_sum.89
  109.1 0.0 all-to-all-done
  109.1 0.7 reduce_sum.82
  109.8 8.1 %all-gather.14.cloned.1.call-done = f32[64,16,256]{2,1,0:T(8,128)} async-done(((f32[2,16,256]{2,1,0:T(8,128)}), f32[64,16,256]{2,1,0:T(8,128)}) %all-gather.14.cloned.1.call-update) | async-done | bytes 1048592 | tf_op jit(solution)/shard_map/all_gather | solution.py:23
  117.8 1.9 %reduce_sum.81 = f32[2,16,256]{2,1,0:T(8,128)} reduce(f32[32,2,16,256]{3,2,1,0:T(8,128)} %bitcast.31, f32[]{:T(128)} %constant.37.clone.1), dimensions={0}, to_apply=%region_0.1 | reduce | flops 253952 | bytes 1081348 | tf_op jit(solution)/shard_map/reduce_sum | solution.py:23
  (8 shorter events, 0.1 us)
Async XLA Ops:
  7.2 6.8 %copy-start.2 = (f32[16,4096]{1,0:T(8,128)S(1)}, f32[16,4096]{1,0:T(8,128)}, u32[]{:S(2)}) copy-start(f32[16,4096]{1,0:T(8,128)} %param.5) | copy-start | bytes 786436
  7.2 110.7 %all-gather.14.cloned.1.call-start = ((), (), s32[]{:S(2)}) async-start(), calls=%async_computation.1 | async-start | bytes 1081344 | tf_op jit(solution)/shard_map/all_gather | solution.py:23
  7.3 6.8 %copy-start = (f32[256,4096]{1,0:T(8,128)S(1)}, f32[256,4096]{1,0:T(8,128)}, u32[]{:S(2)}) copy-start(f32[256,4096]{1,0:T(8,128)} %param.3) | copy-start | bytes 12582916
  58.1 5.0 %copy-start.1 = (f32[256,4096]{1,0:T(8,128)S(1)}, f32[256,4096]{1,0:T(8,128)}, u32[]{:S(2)}) copy-start(f32[256,4096]{1,0:T(8,128)} %param.4) | copy-start | bytes 12582916
  66.7 42.4 %all-to-all-start = ((f32[8,2,16,512]{3,2,1,0:T(8,128)}), f32[8,2,16,512]{3,2,1,0:T(8,128)S(1)}, u32[]{:S(2)}, u32[]{:S(2)}) async-start(f32[8,2,16,512]{3,2,1,0:T(8,128)} %maximum_bitcast_fusion), calls=%async_computation | async-start | bytes 1048576 | tf_op jit(solution)/shard_map/all_to_all | solution.py:34
Sparse Core Ops, SparseCore 0:
  58.2 59.5 all-gather.13
